TPU v7x, 512 devices: a whole 4x4x16 slice. The times are simulated.
512 devices in a mesh: row: 16 (over z), col: 32 (over y, x, core).
Axes of the slice: x: 4, y: 4, z: 16, core: 2. Of those that a mesh axis runs over, the one named last changes fastest.
Arguments:
- right_side: bfloat16 [16384, 16384], P('row', 'col'), may hold values from -180 to 180
- theta_left: bfloat16 [512, 16384], P(None, 'row'), may hold values from -0.125 to 0.125
- theta_right: bfloat16 [512, 16384], P(None, 'col'), may hold values from -0.125 to 0.125
- query_rows: int32 [1024, 2], replicated, may hold values from 0 to 16384, as said below
- query_cols: int32 [1024, 2], replicated, may hold values from 0 to 16384, as said below
Outputs:
- residual: float32 [16384, 16384], P('row', 'col')
- step_ratio: float32 [1], replicated
- answers: float32 [1024], replicated
Inputs may be any that keep to these rules, and one draw needn't show every extreme that they name: `query_rows`: each row is a start and an end with 0 <= start < end <= 16384. `query_cols`: each row is a start and an end with 0 <= start < end <= 16384.
All inputs are finite; a program needn't handle non-finite values.
Results may differ from a plain program's by a relative error of at most 0.0003.
Values sent between devices are 32-bit elements; how exact they have to be, the bound alone decides.
A program may use at most 64 MiB of HBM per device.

v0:
```python
import jax
import jax.numpy as jnp
from jax import lax
from jax.sharding import PartitionSpec as P


def prefix_2(part, axis, combine, identity):
    place = lax.axis_index(axis)
    gathered = lax.all_gather(part, axis)
    state = jnp.zeros_like(part) + jnp.asarray(identity, part.dtype)

    def one(hop, state):
        return combine(state, lax.dynamic_index_in_dim(gathered, hop, 0, False))

    return lax.fori_loop(0, place, one, state)


def add_pair(earlier, later):
    return earlier + later


def cum_last(values):
    length = values.shape[1]
    block_len = 128
    index_line = jnp.arange(block_len)
    upper_tri = (index_line[:, None] <= index_line[None, :]).astype(jnp.float32)
    pieces = values.reshape(values.shape[0], length // block_len, block_len)
    within = jnp.einsum("rbk,kj->rbj", pieces, upper_tri, precision=lax.Precision.HIGHEST)
    totals = within[:, :, -1]
    carried = jnp.cumsum(totals, axis=1) - totals
    return (within + carried[:, :, None]).reshape(values.shape)


def cum_first(values):
    length = values.shape[0]
    block_len = 128
    index_line = jnp.arange(block_len)
    lower_tri = (index_line[:, None] >= index_line[None, :]).astype(jnp.float32)
    pieces = values.reshape(length // block_len, block_len, values.shape[1])
    within = jnp.einsum("ik,bkc->bic", lower_tri, pieces, precision=lax.Precision.HIGHEST)
    totals = within[:, -1, :]
    carried = jnp.cumsum(totals, axis=0) - totals
    return (within + carried[:, None, :]).reshape(values.shape)


def down_scan(column_totals):
    return prefix_2(column_totals, "row", add_pair, jnp.zeros_like(column_totals))


def shards(right_side, theta_left, theta_right, query_rows, query_cols):
    highest = lax.Precision.HIGHEST
    block_rows, block_cols = right_side.shape
    start_field = right_side.astype(jnp.float32)
    left_wide = theta_left.astype(jnp.float32)
    right_wide = theta_right.astype(jnp.float32)
    start_norm = lax.psum(jnp.sum(start_field * start_field), ("row", "col"))
    partial_right = lax.dot_general(
        right_side, theta_right, (((1,), (1,)), ((), ())), preferred_element_type=jnp.float32
    )
    summed_right = lax.psum(partial_right, "col")
    middle = start_field + jnp.dot(
        summed_right, right_wide, precision=highest, preferred_element_type=jnp.float32
    )
    partial_left = jnp.dot(left_wide, middle, precision=highest, preferred_element_type=jnp.float32)
    summed_left = lax.psum(partial_left, "row")
    image_field = middle + lax.dot_general(
        left_wide,
        summed_left,
        (((0,), (0,)), ((), ())),
        precision=highest,
        preferred_element_type=jnp.float32,
    )
    curvature = lax.psum(jnp.sum(start_field * image_field), ("row", "col"))
    alpha_step = start_norm / curvature
    residual = start_field - alpha_step * image_field
    fresh = lax.psum(jnp.sum(residual * residual), ("row", "col"))
    step_ratio = (fresh / start_norm).reshape(1)
    solution = alpha_step * start_field
    across = cum_last(solution)
    row_totals = across[:, -1]
    left_carry = prefix_2(row_totals, "col", add_pair, jnp.zeros_like(row_totals))
    vertical = cum_first(across + left_carry[:, None])
    upper_carry = down_scan(vertical[-1, :])
    prefix = vertical + upper_carry[None, :]
    row_start = lax.axis_index("row") * block_rows
    col_start = lax.axis_index("col") * block_cols
    flat_prefix = prefix.reshape(-1)

    def corner_value(row_bound, col_bound):
        local_row = row_bound - 1 - row_start
        local_col = col_bound - 1 - col_start
        inside = (
            (local_row >= 0)
            & (local_row < block_rows)
            & (local_col >= 0)
            & (local_col < block_cols)
        )
        position_flat = jnp.clip(local_row, 0, block_rows - 1) * block_cols + jnp.clip(
            local_col, 0, block_cols - 1
        )
        return jnp.where(inside, jnp.take(flat_prefix, position_flat), 0.0)

    low_row = query_rows[:, 0]
    high_row = query_rows[:, 1]
    low_col = query_cols[:, 0]
    high_col = query_cols[:, 1]
    partial_answers = (
        corner_value(high_row, high_col)
        - corner_value(low_row, high_col)
        - corner_value(high_row, low_col)
        + corner_value(low_row, low_col)
    )
    combined = lax.psum(partial_answers, ("row", "col"))
    area = (high_row - low_row).astype(jnp.float32) * (high_col - low_col).astype(jnp.float32)
    answers = combined / jnp.sqrt(area)
    return (residual, step_ratio, answers)


def solution(mesh):
    return jax.shard_map(
        shards,
        mesh=mesh,
        in_specs=(P("row", "col"), P(None, "row"), P(None, "col"), P(), P()),
        out_specs=(P("row", "col"), P(), P()),
        check_vma=False,
    )
```

profile of v0, /device:TPU:1, one launch (start us, length us, event | category | flops | bytes accessed | tf_op | source)
XLA Modules:
  0.0 611.5 jit_solution(15123079067743380518)
XLA Ops:
  7.2 0.0 copy-start
  7.2 0.0 copy-start.1
  7.2 0.0 copy-start.2
  7.2 0.0 all-reduce.5.cloned.1.call-start
  7.2 3.5 fusion.25
  10.7 0.0 all-reduce.5.cloned.1.call-update
  10.8 0.0 all-reduce.7.cloned.1.call-start
  10.8 0.0 copy-done.1
  10.8 0.0 copy-done.2
  10.9 144.4 %all-reduce.5.cloned.1.call-done = f32[1024,512]{1,0:T(8,128)} async-done(((f32[1024,512]{1,0:T(8,128)}), f32[1024,512]{1,0:T(8,128)}) %all-reduce.5.cloned.1.call-update) | async-done | bytes 2097168 | tf_op jit(solution)/shard_map/psum | solution.py:60
  155.3 3.8 convert_add_fusion
  159.1 0.0 copy-done
  159.2 4.4 convolution_bitcast_fusion
  163.6 0.0 all-reduce.7.cloned.1.call-update
  163.6 0.6 fusion.21
  164.2 0.7 and_reduce_fusion.3
  164.9 0.6 fusion.22
  165.5 0.6 fusion.23
  166.1 0.6 fusion.24
  166.7 0.6 multiply_rsqrt_fusion
  167.3 125.6 %all-reduce.7.cloned.1.call-done = f32[512,512]{0,1:T(8,128)} async-done(((f32[512,512]{0,1:T(8,128)}), f32[512,512]{0,1:T(8,128)}) %all-reduce.7.cloned.1.call-update) | async-done | bytes 1048592 | tf_op jit(solution)/shard_map/psum | solution.py:65
  292.9 5.5 fusion.1
  298.4 110.7 %all-reduce.1 = (f32[]{:T(128)}, f32[]{:T(128)}) all-reduce(f32[]{:T(128)} %get-tuple-element.53, f32[]{:T(128)} %get-tuple-element.52), channel_id=1, replica_groups=mesh['row'=16,'col'=32] {'row','col'}, use_global_device_ids=true, to_apply=%region_1.0 | all-reduce | flops 2 | bytes 16 | tf_op jit(solution)/shard_map/psum | solution.py:56
  410.4 4.5 multiply_reduce_fusion
  414.9 1.2 fusion.3
  416.2 0.3 broadcast_add_fusion.1
  416.5 24.4 %all-gather = f32[32768,1]{0,1:T(1,128)S(1)} all-gather(f32[1024,1]{0,1:T(1,128)S(1)} %slice.41), channel_id=2, replica_groups=mesh['row'=16,'col'=32] {'col'}, dimensions={0}, use_global_device_ids=true | all-gather | bytes 135168 | tf_op jit(solution)/shard_map/all_gather | solution.py:9
  440.9 0.5 broadcast.172
  441.5 0.9 reduce.11
  442.4 0.1 while.20
  442.4 1.8 copy.22
  444.3 1.9 copy.16
  446.2 1.4 fusion.8
  447.7 0.2 broadcast_add_fusion
  447.9 19.9 %all-gather.1 = f32[16,1,512]{2,1,0:T(1,128)S(1)} all-gather(f32[1,1,512]{2,1,0:T(1,128)S(1)} %slice_bitcast_fusion), channel_id=1, replica_groups=mesh['row'=16,'col'=32] {'row'}, dimensions={0}, use_global_device_ids=true | all-gather | bytes 34816 | tf_op jit(solution)/shard_map/all_gather | solution.py:9
  467.9 0.3 broadcast_bitcast_fusion
  468.1 0.5 copy.24
  468.7 0.5 copy.23
  469.2 0.0 copy-start.4
  469.2 0.2 add.122
  469.5 0.5 copy-done.4
  469.9 6.1 %gather_fusion = f32[1024]{0:T(1024)S(1)} fusion(f32[524288]{0:T(1024)S(1)} %add.122, s32[1024]{0:T(1024)S(1)} %copy-done.4), kind=kCustom, calls=%fused_computation.clone | custom fusion | bytes 12288 | tf_op jit(solution)/shard_map/jit(_take)/gather | solution.py:101
  476.1 6.2 %gather_fusion.1 = f32[1024]{0:T(1024)S(1)} fusion(f32[524288]{0:T(1024)S(1)} %add.122, s32[1024]{0:T(1024)S(1)} %copy-done.7), kind=kCustom, calls=%fused_computation.1.clone | custom fusion | bytes 12288 | tf_op jit(solution)/shard_map/jit(_take)/gather | solution.py:101
  482.3 0.0 copy-start.6
  482.3 6.2 %gather_fusion.2 = f32[1024]{0:T(1024)S(1)} fusion(f32[524288]{0:T(1024)S(1)} %add.122, s32[1024]{0:T(1024)S(1)} %copy-done.5), kind=kCustom, calls=%fused_computation.2.clone | custom fusion | bytes 12288 | tf_op jit(solution)/shard_map/jit(_take)/gather | solution.py:101
  488.5 6.2 %gather_fusion.3 = f32[1024]{0:T(1024)S(1)} fusion(f32[524288]{0:T(1024)S(1)} %add.122, s32[1024]{0:T(1024)S(1)} %copy-done.6), kind=kCustom, calls=%fused_computation.3.clone | custom fusion | bytes 12288 | tf_op jit(solution)/shard_map/jit(_take)/gather | solution.py:101
  494.7 106.9 %all-reduce = (f32[]{:T(128)}, f32[1024]{0:T(1024)S(1)}) all-reduce(f32[]{:T(128)} %get-tuple-element.78, f32[1024]{0:T(1024)S(1)} %fusion.18), channel_id=1, replica_groups=mesh['row'=16,'col'=32] {'row','col'}, use_global_device_ids=true, to_apply=%region_7.0 | all-reduce | flops 1025 | bytes 8200 | tf_op jit(solution)/shard_map/psum | solution.py:76
  602.9 0.6 div.11
  (30 shorter events, 0.2 us)
Async XLA Ops:
  7.2 152.0 %copy-start = (bf16[512,1024]{1,0:T(8,128)(2,1)S(1)}, bf16[512,1024]{1,0:T(8,128)(2,1)}, u32[]{:S(2)}) copy-start(bf16[512,1024]{1,0:T(8,128)(2,1)} %param.12) | copy-start | bytes 3145732
  7.2 3.6 copy-start.1
  7.2 3.6 copy-start.2
  7.2 148.1 %all-reduce.5.cloned.1.call-start = ((), (), s32[]{:S(2)}) async-start(), calls=%async_computation | async-start | bytes 4194304 | tf_op jit(solution)/shard_map/psum | solution.py:60
  10.8 282.2 %all-reduce.7.cloned.1.call-start = ((), (), s32[]{:S(2)}) async-start(), calls=%async_computation.1 | async-start | bytes 2097152 | tf_op jit(solution)/shard_map/psum | solution.py:65
  469.2 0.7 copy-start.4
  469.9 6.2 %copy-start.7 = (s32[1024]{0:T(1024)S(1)}, s32[1024]{0:T(1024)}, u32[]{:S(2)}) copy-start(s32[1024]{0:T(1024)} %fusion.22) | copy-start | bytes 12292
  476.1 6.2 %copy-start.5 = (s32[1024]{0:T(1024)S(1)}, s32[1024]{0:T(1024)}, u32[]{:S(2)}) copy-start(s32[1024]{0:T(1024)} %fusion.23) | copy-start | bytes 12292
  482.3 6.2 %copy-start.6 = (s32[1024]{0:T(1024)S(1)}, s32[1024]{0:T(1024)}, u32[]{:S(2)}) copy-start(s32[1024]{0:T(1024)} %fusion.24) | copy-start | bytes 12292
  488.4 6.2 %copy-start.8 = (pred[1024]{0:T(1024)(128)(4,1)S(1)}, pred[1024]{0:T(1024)(128)(4,1)}, u32[]{:S(2)}) copy-start(pred[1024]{0:T(1024)(128)(4,1)} %get-tuple-element.54) | copy-start | bytes 3076
  488.5 6.2 %copy-start.9 = (pred[1024]{0:T(1024)(128)(4,1)S(1)}, pred[1024]{0:T(1024)(128)(4,1)}, u32[]{:S(2)}) copy-start(pred[1024]{0:T(1024)(128)(4,1)} %get-tuple-element.55) | copy-start | bytes 3076
  488.5 6.2 %copy-start.10 = (pred[1024]{0:T(1024)(128)(4,1)S(1)}, pred[1024]{0:T(1024)(128)(4,1)}, u32[]{:S(2)}) copy-start(pred[1024]{0:T(1024)(128)(4,1)} %get-tuple-element.56) | copy-start | bytes 3076
  488.5 6.2 %copy-start.11 = (pred[1024]{0:T(1024)(128)(4,1)S(1)}, pred[1024]{0:T(1024)(128)(4,1)}, u32[]{:S(2)}) copy-start(pred[1024]{0:T(1024)(128)(4,1)} %get-tuple-element.57) | copy-start | bytes 3076
  488.5 114.4 %copy-start.3 = (f32[1024,1]{0,1:T(1,128)S(1)}, f32[1024,1]{0,1:T(1,128)}, u32[]{:S(2)}) copy-start(f32[1024,1]{0,1:T(1,128)} %multiply_rsqrt_fusion) | copy-start | bytes 12292
Sparse Core Ops, SparseCore 0:
  11.9 143.3 all-reduce.4
  163.7 129.1 all-reduce.6
where the time goes:
time: 612 us
  waiting for transfers between devices  270 us (44%)
  blocking collectives  262 us (43%)
  local copies, waits for them, and re-layouts  30.8 us (5%)
  matrix products  19.9 us (3%)
  between operations  18.2 us (3%)
  other arithmetic  10.5 us (2%)
    psum x1, waiting for transfers between devices, shards(): summed_right = lax.psum(partial_right, 'col')  144 us
    psum x1, waiting for transfers between devices, shards(): summed_left = lax.psum(partial_left, 'row')  126 us
    psum x1, blocking collectives, shards(): start_norm = lax.psum(jnp.sum(start_field * start_field), ('row', 'col'))  111 us
    psum x1, blocking collectives, shards(): fresh = lax.psum(jnp.sum(residual * residual), ('row', 'col'))  107 us
    all_gather x2, blocking collectives, prefix_2(): gathered = lax.all_gather(part, axis)  44.4 us
    gather x4, local copies, waits for them, and re-layouts, corner_value(): return jnp.where(inside, jnp.take(flat_prefix, position_flat), 0.0)  24.6 us
  transfers between devices with their start and end apart: 2, of which 2 were waited for; matrix products, arithmetic and copies ran while one was open for 1% of the time, Pallas kernels for 0%

commit v1 on v0

--- a/solution.py
+++ b/solution.py
@@ -1,7 +1,22 @@
+import functools
 import jax
 import jax.numpy as jnp
 from jax import lax
 from jax.sharding import PartitionSpec as P
+
+
+def _plan_spans(t0, dev_axis):
+    extent = lax.axis_size(dev_axis)
+    row_out = lambda b_now: [(hop_no, hop_no ^ b_now) for hop_no in range(extent)]
+    new = t0
+    for dev_i in range(extent.bit_length() - 1):
+        t1 = row_out(1 << dev_i)
+        res = lax.ppermute(new, dev_axis, perm=t1)
+        new = new + res
+    return new
+
+
+resolve_the_corner = functools.partial(_plan_spans, dev_axis="col")
 
 
 def prefix_2(part, axis, combine, identity):
@@ -57,7 +72,7 @@
     partial_right = lax.dot_general(
         right_side, theta_right, (((1,), (1,)), ((), ())), preferred_element_type=jnp.float32
     )
-    summed_right = lax.psum(partial_right, "col")
+    summed_right = resolve_the_corner(partial_right)
     middle = start_field + jnp.dot(
         summed_right, right_wide, precision=highest, preferred_element_type=jnp.float32
     )

time: 612 us -> 678 us (1.11)
  waiting for transfers between devices: 270 us -> 320 us
  starting transfers between devices: 0.08 us -> 16.5 us
    ppermute x0 -> x5, waiting for transfers between devices: none -> 188 us  [_plan_spans(): res = lax.ppermute(new, dev_axis, perm=t1)]
    psum x1 -> x0, waiting for transfers between devices: 144 us -> none  [shards(): summed_right = lax.psum(partial_right, 'col')]
    ppermute x0 -> x5, starting transfers between devices: none -> 16.5 us  [_plan_spans(): res = lax.ppermute(new, dev_axis, perm=t1)]
  transfers between devices with their start and end apart: 2 -> 6, of which waited for: 2 -> 6; matrix products, arithmetic and copies ran while one was open for 1% -> 0% of each run, Pallas kernels for 0% -> 0%
where the time goes in v1:
time: 678 us
  waiting for transfers between devices  320 us (47%)
  blocking collectives  262 us (39%)
  local copies, waits for them, and re-layouts  31.3 us (5%)
  matrix products  20.8 us (3%)
  between operations  18.2 us (3%)
  starting transfers between devices  16.5 us (2%)
  other arithmetic  8.92 us (1%)
    ppermute x5, waiting for transfers between devices, _plan_spans(): res = lax.ppermute(new, dev_axis, perm=t1)  188 us
    psum x1, waiting for transfers between devices, shards(): summed_left = lax.psum(partial_left, 'row')  132 us
    psum x1, blocking collectives, shards(): start_norm = lax.psum(jnp.sum(start_field * start_field), ('row', 'col'))  111 us
    psum x1, blocking collectives, shards(): fresh = lax.psum(jnp.sum(residual * residual), ('row', 'col'))  107 us
    all_gather x2, blocking collectives, prefix_2(): gathered = lax.all_gather(part, axis)  44.1 us
    gather x4, local copies, waits for them, and re-layouts, corner_value(): return jnp.where(inside, jnp.take(flat_prefix, position_flat), 0.0)  24.6 us
    ppermute x5, starting transfers between devices, _plan_spans(): res = lax.ppermute(new, dev_axis, perm=t1)  16.5 us
  transfers between devices with their start and end apart: 6, of which 6 were waited for; matrix products, arithmetic and copies ran while one was open for 0% of the time, Pallas kernels for 0%

profile of v1, /device:TPU:1, one launch (start us, length us, event | category | flops | bytes accessed | tf_op | source)
XLA Modules:
  0.0 677.8 jit_solution(13868598141088137733)
XLA Ops:
  7.2 0.0 copy-start
  7.2 0.0 all-reduce.4.cloned.1.call-start
  7.2 2.2 fusion.29
  9.4 8.8 %collective-permute-start = (f32[1024,512]{1,0:T(8,128)S(1)}, f32[1024,512]{1,0:T(8,128)S(1)}, u32[]{:S(2)}, u32[]{:S(2)}) collective-permute-start(f32[1024,512]{1,0:T(8,128)S(1)} %fusion.29), channel_id=1, source_target_pairs={{0,1},{1,0},{2,3},{3,2},{4,5},{5,4},{6,7},{7,6},{8,9},{9,8},{10,11... | collective-permute-start | bytes 6291464 | tf_op jit(solution)/shard_map/ppermute | solution.py:14
  18.2 3.8 collective-permute-done
  22.0 0.5 add.122
  22.4 1.9 collective-permute-start.1
  24.4 46.8 %collective-permute-done.1 = f32[1024,512]{1,0:T(8,128)S(1)} collective-permute-done((f32[1024,512]{1,0:T(8,128)S(1)}, f32[1024,512]{1,0:T(8,128)S(1)}, u32[]{:S(2)}, u32[]{:S(2)}) %collective-permute-start.1) | collective-permute-done | bytes 2097184 | tf_op jit(solution)/shard_map/ppermute | solution.py:14
  71.2 0.5 add.123
  71.7 1.9 collective-permute-start.2
  73.6 47.4 %collective-permute-done.2 = f32[1024,512]{1,0:T(8,128)S(1)} collective-permute-done((f32[1024,512]{1,0:T(8,128)S(1)}, f32[1024,512]{1,0:T(8,128)S(1)}, u32[]{:S(2)}, u32[]{:S(2)}) %collective-permute-start.2) | collective-permute-done | bytes 2097184 | tf_op jit(solution)/shard_map/ppermute | solution.py:14
  121.0 0.5 add.124
  121.5 0.0 copy-start.3
  121.5 1.9 collective-permute-start.3
  123.4 45.0 %collective-permute-done.3 = f32[1024,512]{1,0:T(8,128)S(1)} collective-permute-done((f32[1024,512]{1,0:T(8,128)S(1)}, f32[1024,512]{1,0:T(8,128)S(1)}, u32[]{:S(2)}, u32[]{:S(2)}) %collective-permute-start.3) | collective-permute-done | bytes 2097184 | tf_op jit(solution)/shard_map/ppermute | solution.py:14
  168.4 0.5 add.125
  168.9 0.0 copy-start.1
  168.9 1.9 collective-permute-start.4
  170.9 45.6 %collective-permute-done.4 = f32[1024,512]{1,0:T(8,128)} collective-permute-done((f32[1024,512]{1,0:T(8,128)S(1)}, f32[1024,512]{1,0:T(8,128)}, u32[]{:S(2)}, u32[]{:S(2)}) %collective-permute-start.4) | collective-permute-done | bytes 2097184 | tf_op jit(solution)/shard_map/ppermute | solution.py:14
  216.5 4.5 convert_add_fusion
  220.9 4.4 convolution_bitcast_fusion
  225.4 0.0 all-reduce.4.cloned.1.call-update
  225.4 0.1 and_reduce_fusion.3
  225.6 131.6 %all-reduce.4.cloned.1.call-done = f32[512,512]{0,1:T(8,128)} async-done(((f32[512,512]{0,1:T(8,128)}), f32[512,512]{0,1:T(8,128)}) %all-reduce.4.cloned.1.call-update) | async-done | bytes 1048592 | tf_op jit(solution)/shard_map/psum | solution.py:80
  357.2 5.5 fusion.1
  362.6 110.9 %all-reduce.1 = (f32[]{:T(128)}, f32[]{:T(128)}) all-reduce(f32[]{:T(128)} %get-tuple-element.53, f32[]{:T(128)} %get-tuple-element.52), channel_id=1, replica_groups=mesh['row'=16,'col'=32] {'row','col'}, use_global_device_ids=true, to_apply=%region_1.0 | all-reduce | flops 2 | bytes 16 | tf_op jit(solution)/shard_map/psum | solution.py:71
  474.9 4.5 multiply_reduce_fusion
  479.4 1.2 fusion.3
  480.6 0.3 broadcast_add_fusion.1
  480.9 1.8 copy.22
  482.7 3.0 copy.16
  485.7 24.2 %all-gather = f32[32768,1]{0,1:T(1,128)S(1)} all-gather(f32[1024,1]{0,1:T(1,128)S(1)} %slice.41), channel_id=2, replica_groups=mesh['row'=16,'col'=32] {'col'}, dimensions={0}, use_global_device_ids=true | all-gather | bytes 135168 | tf_op jit(solution)/shard_map/all_gather | solution.py:24
  509.9 0.5 broadcast.172
  510.4 0.9 reduce.11
  511.4 0.1 while.20
  511.5 3.0 fusion.12
  514.6 0.2 broadcast_add_fusion
  514.8 19.9 %all-gather.1 = f32[16,1,512]{2,1,0:T(1,128)S(1)} all-gather(f32[1,1,512]{2,1,0:T(1,128)S(1)} %slice_bitcast_fusion), channel_id=1, replica_groups=mesh['row'=16,'col'=32] {'row'}, dimensions={0}, use_global_device_ids=true | all-gather | bytes 34816 | tf_op jit(solution)/shard_map/all_gather | solution.py:24
  534.7 0.3 broadcast_bitcast_fusion
  535.0 0.5 copy.24
  535.5 0.5 copy.23
  536.1 0.2 add.140
  536.3 6.2 gather_fusion
  542.5 6.2 gather_fusion.1
  548.6 6.2 gather_fusion.2
  554.8 6.2 gather_fusion.3
  561.0 106.9 %all-reduce = (f32[]{:T(128)}, f32[1024]{0:T(1024)S(1)}) all-reduce(f32[]{:T(128)} %get-tuple-element.78, f32[1024]{0:T(1024)S(1)} %fusion.22), channel_id=1, replica_groups=mesh['row'=16,'col'=32] {'row','col'}, use_global_device_ids=true, to_apply=%region_6.0 | all-reduce | flops 1025 | bytes 8200 | tf_op jit(solution)/shard_map/psum | solution.py:91
  669.2 0.6 div.11
  (25 shorter events, 0.2 us)
Async XLA Ops:
  7.2 213.8 %copy-start = (bf16[512,1024]{1,0:T(8,128)(2,1)S(1)}, bf16[512,1024]{1,0:T(8,128)(2,1)}, u32[]{:S(2)}) copy-start(bf16[512,1024]{1,0:T(8,128)(2,1)} %param.12) | copy-start | bytes 3145732
  7.2 350.0 %all-reduce.4.cloned.1.call-start = ((), (), s32[]{:S(2)}) async-start(), calls=%async_computation | async-start | bytes 2097152 | tf_op jit(solution)/shard_map/psum | solution.py:80
  9.4 12.6 %collective-permute-start = (f32[1024,512]{1,0:T(8,128)S(1)}, f32[1024,512]{1,0:T(8,128)S(1)}, u32[]{:S(2)}, u32[]{:S(2)}) collective-permute-start(f32[1024,512]{1,0:T(8,128)S(1)} %fusion.29), channel_id=1, source_target_pairs={{0,1},{1,0},{2,3},{3,2},{4,5},{5,4},{6,7},{7,6},{8,9},{9,8},{10,11... | collective-permute-start | bytes 6291464 | tf_op jit(solution)/shard_map/ppermute | solution.py:14
  22.4 48.7 %collective-permute-start.1 = (f32[1024,512]{1,0:T(8,128)S(1)}, f32[1024,512]{1,0:T(8,128)S(1)}, u32[]{:S(2)}, u32[]{:S(2)}) collective-permute-start(f32[1024,512]{1,0:T(8,128)S(1)} %add.122), channel_id=1, source_target_pairs={{0,2},{1,3},{2,0},{3,1},{4,6},{5,7},{6,4},{7,5},{8,10},{9,11},{10,... | collective-permute-start | bytes 6291464 | tf_op jit(solution)/shard_map/ppermute | solution.py:14
  71.7 49.3 %collective-permute-start.2 = (f32[1024,512]{1,0:T(8,128)S(1)}, f32[1024,512]{1,0:T(8,128)S(1)}, u32[]{:S(2)}, u32[]{:S(2)}) collective-permute-start(f32[1024,512]{1,0:T(8,128)S(1)} %add.123), channel_id=1, source_target_pairs={{0,4},{1,5},{2,6},{3,7},{4,0},{5,1},{6,2},{7,3},{8,12},{9,13},{10,... | collective-permute-start | bytes 6291464 | tf_op jit(solution)/shard_map/ppermute | solution.py:14
  121.5 49.3 %copy-start.2 = (s32[1024,2]{0,1:T(2,128)S(1)}, s32[1024,2]{0,1:T(2,128)}, u32[]{:S(2)}) copy-start(s32[1024,2]{0,1:T(2,128)} %param.14) | copy-start | bytes 24580
  121.5 49.3 %copy-start.3 = (s32[1024,2]{0,1:T(2,128)S(1)}, s32[1024,2]{0,1:T(2,128)}, u32[]{:S(2)}) copy-start(s32[1024,2]{0,1:T(2,128)} %param.15) | copy-start | bytes 24580
  121.5 46.9 %collective-permute-start.3 = (f32[1024,512]{1,0:T(8,128)S(1)}, f32[1024,512]{1,0:T(8,128)S(1)}, u32[]{:S(2)}, u32[]{:S(2)}) collective-permute-start(f32[1024,512]{1,0:T(8,128)S(1)} %add.124), channel_id=1, source_target_pairs={{0,8},{1,9},{2,10},{3,11},{4,12},{5,13},{6,14},{7,15},{8,0},{9,1},... | collective-permute-start | bytes 6291464 | tf_op jit(solution)/shard_map/ppermute | solution.py:14
  168.9 2.0 copy-start.1
  168.9 47.6 %collective-permute-start.4 = (f32[1024,512]{1,0:T(8,128)S(1)}, f32[1024,512]{1,0:T(8,128)}, u32[]{:S(2)}, u32[]{:S(2)}) collective-permute-start(f32[1024,512]{1,0:T(8,128)S(1)} %add.125), channel_id=1, source_target_pairs={{0,16},{1,17},{2,18},{3,19},{4,20},{5,21},{6,22},{7,23},{8,24},{9,... | collective-permute-start | bytes 6291464 | tf_op jit(solution)/shard_map/ppermute | solution.py:14
Sparse Core Ops, SparseCore 0:
  225.5 131.5 all-reduce.3
